TPU v7x, 32 devices: a whole 2x2x4 slice. The times are simulated.
32 devices in a mesh: mem: 8 (over y, x, core), band: 4 (over z).
Axes of the slice: x: 2, y: 2, z: 4, core: 2. Of those that a mesh axis runs over, the one named last changes fastest.
Arguments:
- ensemble: bfloat16 [256, 3, 240, 160], P('mem', None, 'band'), may hold values from -8 to 8, as said below
- layer_depth: float32 [240, 160], P('band'), may hold values from 0.5 to 2
- observed_cell: int32 [8, 8, 512], P('mem', 'band'), may hold values from 0 to 1799
- observed_value: float32 [8, 8, 512], P('mem', 'band'), may hold values from -6 to 6
- error_variance: float32 [8, 8, 512], P('mem', 'band'), may hold values from 4 to 64
- observed_count: int32 [8, 8], P('mem', 'band'), may hold values from 256 to 512, as said below
Outputs:
- analysis: bfloat16 [256, 3, 240, 160], P('mem', None, 'band')
Inputs may be any that keep to these rules, and one draw needn't show every extreme that they name: `ensemble`: the forecast members scatter around a common state. `observed_count`: some tile holds 512 observations; the slots from the count on are unused.
All inputs are finite; a program needn't handle non-finite values.
Results may differ from a plain program's by a relative error of at most 0.0051.
The roundings to bfloat16 on the way count: a program that leaves them out, or rounds other values in their place, can miss the bound.
Values may be sent and summed in bfloat16 or wider, within the bound.
No kernel may reach another device: no remote copies, remote signals or barrier semaphores. Data moves between devices by JAX's collectives and lax.ppermute only.
A program may use at most 128 MiB of HBM per device.

v0:
```python
import math
import jax
import jax.numpy as jnp
from jax import lax
from jax.sharding import PartitionSpec as P

SWEEPS = 5
half_step = 0.1
coriolis_scale = 0.3
neighbour_weight = 0.75


def padded_2(cells, sides, width):
    for axis, dim in sides:
        count = lax.axis_size(axis)
        head = lax.slice_in_dim(cells, 0, width, axis=dim)
        tail = lax.slice_in_dim(cells, cells.shape[dim] - width, cells.shape[dim], axis=dim)
        cells = jnp.concatenate(
            [
                lax.ppermute(tail, axis, [(i, (i + 1) % count) for i in range(count)]),
                cells,
                lax.ppermute(head, axis, [((i + 1) % count, i) for i in range(count)]),
            ],
            axis=dim,
        )
    return cells


def north_south(source):
    widths = [(0, 0)] * (source.ndim - 1) + [(1, 1)]
    padded = jnp.pad(source, widths)
    return padded[..., 2:] - padded[..., :-2]


def coriolis(latitudes):
    position = jnp.arange(latitudes, dtype=jnp.float32)
    return coriolis_scale * jnp.sin(math.pi * ((position + 0.5) / latitudes - 0.5))


def newton_schulz(starting):
    identity = jnp.eye(starting.shape[-1], dtype=starting.dtype)
    root_part = starting
    inverse_root = jnp.broadcast_to(identity, starting.shape)
    for sweep_index in range(SWEEPS):
        product = jnp.einsum(
            "tij,tjk->tik", inverse_root, root_part, precision=lax.Precision.HIGHEST
        )
        middle = 1.5 * identity - 0.5 * product
        root_part = jnp.einsum("tij,tjk->tik", root_part, middle, precision=lax.Precision.HIGHEST)
        inverse_root = jnp.einsum(
            "tij,tjk->tik", middle, inverse_root, precision=lax.Precision.HIGHEST
        )
    return inverse_root


def on_device(ensemble, layer_depth, observed_cell, observed_value, error_variance, observed_count):
    block_members = ensemble.shape[0]
    columns = ensemble.shape[2]
    latitudes = ensemble.shape[3]
    strips = lax.axis_size("mem")
    members = block_members * strips
    strip_rows = latitudes // strips
    tile_count = observed_cell.shape[1]
    tile_columns = columns // tile_count
    slot_count = observed_cell.shape[2]
    tile_cells = 3 * tile_columns * strip_rows
    height = ensemble[:, 0].astype(jnp.float32)
    eastward = ensemble[:, 1].astype(jnp.float32)
    northward = ensemble[:, 2].astype(jnp.float32)
    turning = coriolis(latitudes)
    flux_east = (layer_depth * eastward).astype(jnp.bfloat16)
    flux_north = (layer_depth * northward).astype(jnp.bfloat16)
    east_margin = padded_2(flux_east, (("band", 1),), 1)
    east_west = east_margin[:, 2:].astype(jnp.float32) - east_margin[:, :-2].astype(jnp.float32)
    north_local = lax.optimization_barrier(flux_north).astype(jnp.float32)
    raised = height - half_step * (east_west + north_south(north_local))
    surface_elevation_cast = raised.astype(jnp.bfloat16)
    height_margin = padded_2(surface_elevation_cast, (("band", 1),), 1)
    margin_wide = height_margin.astype(jnp.float32)
    height_inner = margin_wide[:, 1:-1]
    revised_zonal_velocity = (
        eastward + turning * northward - half_step * (margin_wide[:, 2:] - margin_wide[:, :-2])
    )
    revised_meridional_velocity = (
        northward - turning * eastward - half_step * north_south(height_inner)
    )
    advance_dynamics = jnp.stack(
        [
            surface_elevation_cast,
            revised_zonal_velocity.astype(jnp.bfloat16),
            revised_meridional_velocity.astype(jnp.bfloat16),
        ],
        axis=1,
    )
    reordered = advance_dynamics.reshape(
        block_members, 3, tile_count, tile_columns, strips, strip_rows
    )
    reordered = jnp.transpose(reordered, (4, 2, 0, 1, 3, 5)).reshape(
        strips, tile_count, block_members, tile_cells
    )
    tile_block = lax.all_to_all(reordered, "mem", split_axis=0, concat_axis=2, tiled=True)[0]
    cells_here = observed_cell[0]
    values = jnp.take_along_axis(tile_block, cells_here[:, None, :], axis=2)
    observed_mean = jnp.sum(values, axis=1, dtype=jnp.float32) / members
    slot_index = jnp.arange(slot_count, dtype=jnp.int32)[None, :]
    live_slots = slot_index < observed_count[0][:, None]
    root_weight = jnp.sqrt(jnp.where(live_slots, 1.0 / error_variance[0], 0.0))
    spread = (
        root_weight[:, None, :] * (values.astype(jnp.float32) - observed_mean[:, None, :])
    ).astype(jnp.bfloat16)
    misfit = (root_weight * (observed_value[0] - observed_mean)).astype(jnp.bfloat16)
    spread_margin, misfit_margin = (
        padded_2(spread[None], (("mem", 0), ("band", 1)), 1),
        padded_2(misfit[None], (("mem", 0), ("band", 1)), 1),
    )
    gram_margin = jnp.einsum(
        "atko,atlo->atkl", spread_margin, spread_margin, preferred_element_type=jnp.float32
    )
    pull_margin = jnp.einsum(
        "atko,ato->atk", spread_margin, misfit_margin, preferred_element_type=jnp.float32
    )
    strip_here = lax.axis_index("mem")
    lower_valid = (strip_here > 0).astype(jnp.float32)
    upper_valid = (strip_here < strips - 1).astype(jnp.float32)
    strip_mask = (lower_valid, 1.0, upper_valid)
    total_gram = jnp.zeros((tile_count, members, members), jnp.float32)
    total_pull = jnp.zeros((tile_count, members), jnp.float32)
    for offset_lat in range(3):
        for offset_lon in range(3):
            factor = (
                neighbour_weight ** (abs(offset_lat - 1) + abs(offset_lon - 1))
                * strip_mask[offset_lat]
            )
            total_gram = (
                total_gram + factor * gram_margin[offset_lat, offset_lon : offset_lon + tile_count]
            )
            total_pull = (
                total_pull + factor * pull_margin[offset_lat, offset_lon : offset_lon + tile_count]
            )
    system = (members - 1) * jnp.eye(members, dtype=jnp.float32)[None] + total_gram
    frobenius = jnp.sqrt(jnp.sum(system * system, axis=(1, 2)))
    inverse_root = newton_schulz(system / frobenius[:, None, None])
    spread_map = inverse_root * (math.sqrt(members - 1) / jnp.sqrt(frobenius))[:, None, None]
    half_pull = jnp.einsum("tij,tj->ti", inverse_root, total_pull, precision=lax.Precision.HIGHEST)
    shift_weights = (
        jnp.einsum("tij,tj->ti", inverse_root, half_pull, precision=lax.Precision.HIGHEST)
        / frobenius[:, None]
    )
    weights = (spread_map + shift_weights[:, :, None]).astype(jnp.bfloat16)
    state_mean = jnp.sum(tile_block, axis=1, dtype=jnp.float32) / members
    anomaly = (tile_block.astype(jnp.float32) - state_mean[:, None, :]).astype(jnp.bfloat16)
    update = jnp.einsum("tjk,tjc->tkc", weights, anomaly, preferred_element_type=jnp.float32)
    analysed = (state_mean[:, None, :] + update).astype(jnp.bfloat16)
    returned = lax.all_to_all(analysed[None], "mem", split_axis=2, concat_axis=0, tiled=True)
    returned = returned.reshape(strips, tile_count, block_members, 3, tile_columns, strip_rows)
    return jnp.transpose(returned, (2, 3, 1, 4, 0, 5)).reshape(block_members, 3, columns, latitudes)


def solution(mesh):
    in_specs = (
        P("mem", None, "band", None),
        P("band", None),
        P("mem", "band", None),
        P("mem", "band", None),
        P("mem", "band", None),
        P("mem", "band"),
    )
    out_specs = P("mem", None, "band", None)
    return jax.shard_map(
        on_device, mesh=mesh, in_specs=in_specs, out_specs=out_specs, check_vma=False
    )
```

profile of v0, /device:TPU:0, one launch (start us, length us, event | category | flops | bytes accessed | tf_op | source)
XLA Modules:
  0.0 279.9 jit_solution(7164611219929606275)
XLA Ops:
  0.0 2.0 fusion.1
  2.1 5.1 %collective-permute-start = (bf16[32,1,160]{2,0,1:T(8,128)(2,1)S(1)}, bf16[32,1,160]{2,0,1:T(8,128)(2,1)S(1)}, u32[]{:S(2)}, u32[]{:S(2)}) collective-permute-start(bf16[32,1,160]{2,0,1:T(8,128)(2,1)S(1)} %get-tuple-element.15), channel_id=1, source_target_pairs={{1,0},{2,1},{3,2},{0,3},{5,4},{6,5},{7,6},{4,7},{9,8},{10,9},{11,1... | collective-permute-start | bytes 30728 | tf_op jit(solution)/shard_map/ppermute | solution.py:22
  7.6 1.0 collective-permute-done
  8.6 4.1 %collective-permute-done.1 = bf16[32,1,160]{2,0,1:T(8,128)(2,1)S(1)} collective-permute-done((bf16[32,1,160]{2,0,1:T(8,128)(2,1)S(1)}, bf16[32,1,160]{2,0,1:T(8,128)(2,1)S(1)}, u32[]{:S(2)}, u32[]{:S(2)}) %collective-permute-start.1) | collective-permute-done | bytes 10272 | tf_op jit(solution)/shard_map/ppermute | solution.py:20
  12.7 2.1 fusion.11
  14.9 3.8 %collective-permute-start.3 = (bf16[32,1,160]{2,0,1:T(8,128)(2,1)S(1)}, bf16[32,1,160]{2,0,1:T(8,128)(2,1)S(1)}, u32[]{:S(2)}, u32[]{:S(2)}) collective-permute-start(bf16[32,1,160]{2,0,1:T(8,128)(2,1)S(1)} %get-tuple-element.14), channel_id=1, source_target_pairs={{1,0},{2,1},{3,2},{0,3},{5,4},{6,5},{7,6},{4,7},{9,8},{10,9},{11,1... | collective-permute-start | bytes 30728 | tf_op jit(solution)/shard_map/ppermute | solution.py:22
  18.8 2.1 copy.30
  20.9 4.6 %stack.12 = bf16[32,1,2,30,8,20]{3,2,5,4,0,1:T(2,128)(2,1)S(1)} reshape(bf16[32,60,160]{1,2,0:T(8,128)(2,1)} %copy.30) | data formatting | bytes 1228800 | tf_op jit(solution)/shard_map/stack | solution.py:87
  25.4 1.5 maximum_convert_fusion
  27.1 1.6 copy-done.2
  28.7 2.6 fusion.3
  31.4 3.0 %copy.31 = bf16[32,60,160]{1,2,0:T(8,128)(2,1)} copy(bf16[32,60,160]{2,0,1:T(8,128)(2,1)} %get-tuple-element.9) | data formatting | bytes 1228800 | tf_op jit(solution)/shard_map/convert_element_type | solution.py:90
  34.4 5.6 %stack.13 = bf16[32,1,2,30,8,20]{3,2,5,4,0,1:T(2,128)(2,1)} reshape(bf16[32,60,160]{1,2,0:T(8,128)(2,1)} %copy.31) | data formatting | bytes 1228800 | tf_op jit(solution)/shard_map/stack | solution.py:87
  40.0 3.1 %copy.32 = bf16[32,60,160]{1,2,0:T(8,128)(2,1)} copy(bf16[32,60,160]{2,0,1:T(8,128)(2,1)} %get-tuple-element.10) | data formatting | bytes 1228800 | tf_op jit(solution)/shard_map/convert_element_type | solution.py:91
  43.1 5.6 %stack.14 = bf16[32,1,2,30,8,20]{3,2,5,4,0,1:T(2,128)(2,1)} reshape(bf16[32,60,160]{1,2,0:T(8,128)(2,1)} %copy.32) | data formatting | bytes 1228800 | tf_op jit(solution)/shard_map/stack | solution.py:87
  48.7 17.0 %maximum_bitcast_fusion = bf16[8,2,32,3,30,20]{4,1,5,0,2,3:T(2,128)(2,1)} fusion(bf16[32,1,2,30,8,20]{3,2,5,4,0,1:T(2,128)(2,1)} %stack.14, bf16[32,1,2,30,8,20]{3,2,5,4,0,1:T(2,128)(2,1)} %stack.13, bf16[32,1,2,30,8,20]{3,2,5,4,0,1:T(2,128)(2,1)S(1)} %stack.12), kind=kLoop, calls=%fused_computation.1 | loop fusion | flops 1843200 | bytes 3686400 | tf_op jit(solution)/shard_map/transpose | solution.py:98
  65.7 24.9 %copy.33 = bf16[8,2,32,3,30,20]{2,0,5,4,3,1:T(8,128)(2,1)} copy(bf16[8,2,32,3,30,20]{4,1,5,0,2,3:T(2,128)(2,1)} %maximum_bitcast_fusion) | data formatting | bytes 3686400 | tf_op jit(solution)/shard_map/transpose | solution.py:98
  90.6 9.1 %copy.34 = bf16[8,2,32,1800]{3,2,1,0:T(8,128)(2,1)} copy(bf16[8,2,32,1800]{2,0,3,1:T(8,128)(2,1)} %bitcast.114) | data formatting | bytes 3686400 | tf_op jit(solution)/shard_map/reshape | solution.py:98
  99.7 4.0 %all-to-all-start = ((bf16[8,2,32,1800]{3,2,1,0:T(8,128)(2,1)}), bf16[8,2,32,1800]{3,2,1,0:T(8,128)(2,1)S(1)}, u32[]{:S(2)}, u32[]{:S(2)}) async-start(bf16[8,2,32,1800]{3,2,1,0:T(8,128)(2,1)} %copy.34), calls=%async_computation | async-start | bytes 3932160 | tf_op jit(solution)/shard_map/all_to_all | solution.py:101
  103.8 25.0 %all-to-all-done = bf16[8,2,32,1800]{3,2,1,0:T(8,128)(2,1)S(1)} async-done(((bf16[8,2,32,1800]{3,2,1,0:T(8,128)(2,1)}), bf16[8,2,32,1800]{3,2,1,0:T(8,128)(2,1)S(1)}, u32[]{:S(2)}, u32[]{:S(2)}) %all-to-all-start) | async-done | bytes 1843232 | tf_op jit(solution)/shard_map/all_to_all | solution.py:101
  128.8 1.5 copy.35
  130.8 2.8 %copy.36 = bf16[2,256,1800]{1,2,0:T(8,128)(2,1)S(1)} copy(bf16[2,256,1800]{2,1,0:T(8,128)(2,1)} %bitcast.118) | data formatting | bytes 3686400 | tf_op jit(solution)/shard_map/squeeze | solution.py:101
  133.6 5.8 %gather_fusion = bf16[1024,256]{1,0:T(8,128)(2,1)S(1)} fusion(bf16[2,256,1800]{1,2,0:T(8,128)(2,1)S(1)} %copy.36, s32[1024]{0:T(1024)S(1)} %bitcast.113), kind=kCustom, calls=%fused_computation | custom fusion | bytes 1056768 | tf_op jit(solution)/shard_map/jit(take_along_axis)/gather | solution.py:103
  140.8 2.3 collective-permute-start.9
  143.0 1.9 convert_reduce_fusion
  144.9 7.6 %collective-permute-done.5 = bf16[1,2,256,512]{3,2,1,0:T(8,128)(2,1)S(1)} collective-permute-done((bf16[1,2,256,512]{3,2,1,0:T(8,128)(2,1)S(1)}, bf16[1,2,256,512]{3,2,1,0:T(8,128)(2,1)S(1)}, u32[]{:S(2)}, u32[]{:S(2)}) %collective-permute-start.5) | collective-permute-done | bytes 524320 | tf_op jit(solution)/shard_map/ppermute | solution.py:22
  152.5 1.1 collective-permute-done.4
  153.9 3.8 %collective-permute-start.7 = (bf16[3,1,256,512]{3,2,1,0:T(8,128)(2,1)S(1)}, bf16[3,1,256,512]{3,2,1,0:T(8,128)(2,1)S(1)}, u32[]{:S(2)}, u32[]{:S(2)}) collective-permute-start(bf16[3,1,256,512]{3,2,1,0:T(8,128)(2,1)S(1)} %get-tuple-element.12), channel_id=1, source_target_pairs={{1,0},{2,1},{3,2},{0,3},{5,4},{6,5},{7,6},{4,7},{9,8},{10,9},{11,1... | collective-permute-start | bytes 2359304 | tf_op jit(solution)/shard_map/ppermute | solution.py:22
  157.9 3.8 %collective-permute-start.11 = (bf16[3,1,512]{2,1,0:T(2,128)(2,1)S(1)}, bf16[3,1,512]{2,1,0:T(2,128)(2,1)S(1)}, u32[]{:S(2)}, u32[]{:S(2)}) collective-permute-start(bf16[3,1,512]{2,1,0:T(2,128)(2,1)S(1)} %get-tuple-element.18), channel_id=1, source_target_pairs={{1,0},{2,1},{3,2},{0,3},{5,4},{6,5},{7,6},{4,7},{9,8},{10,9},{11,1... | collective-permute-start | bytes 9224 | tf_op jit(solution)/shard_map/ppermute | solution.py:22
  161.7 29.6 %collective-permute-done.10 = bf16[3,1,512]{2,1,0:T(2,128)(2,1)S(1)} collective-permute-done((bf16[3,1,512]{2,1,0:T(2,128)(2,1)S(1)}, bf16[3,1,512]{2,1,0:T(2,128)(2,1)S(1)}, u32[]{:S(2)}, u32[]{:S(2)}) %collective-permute-start.10) | collective-permute-done | bytes 3104 | tf_op jit(solution)/shard_map/ppermute | solution.py:20
  191.4 1.3 fusion.58
  193.1 0.7 fusion.17
  193.9 0.7 fusion.35
  195.2 0.7 fusion.16
  195.9 0.7 fusion.65
  196.5 0.7 fusion.64
  197.2 0.7 fusion.15
  199.2 0.7 fusion.14
  199.8 0.7 fusion.68
  201.2 1.3 fusion.36
  202.5 0.7 fusion.13
  203.2 0.7 fusion.70
  205.0 2.2 fusion
  207.2 5.1 %copy.39 = bf16[1,2,256,1800]{3,1,0,2:T(2,128)(2,1)S(1)} copy(bf16[1,2,256,1800]{2,3,1,0:T(8,128)(2,1)} %fusion) | data formatting | bytes 3686400 | tf_op jit(solution)/shard_map/broadcast_in_dim | solution.py:154
  212.3 28.6 %all_to_all.30 = bf16[1,2,256,1800]{3,1,0,2:T(2,128)(2,1)S(1)} all-to-all(bf16[1,2,256,1800]{3,1,0,2:T(2,128)(2,1)S(1)} %copy.39), channel_id=1, replica_groups=mesh['mem'=8,'band'=4] {'mem'}, dimensions={2} | all-to-all | bytes 3686400 | tf_op jit(solution)/shard_map/all_to_all | solution.py:154
  241.1 7.6 %copy.41 = bf16[8,1,2,32,1800]{3,0,4,2,1:T(8,128)(2,1)} copy(bf16[8,1,2,32,1800]{4,3,0,2,1:T(8,128)(2,1)S(1)} %bitcast.117) | data formatting | bytes 3686400 | tf_op jit(solution)/shard_map/all_to_all | solution.py:154
  248.6 16.8 %copy.50 = bf16[32,3,2,30,8,20]{5,4,0,3,2,1:T(8,128)(2,1)} copy(bf16[32,3,2,30,8,20]{0,4,5,3,1,2:T(8,128)(2,1)} %bitcast.115) | data formatting | bytes 3686400 | tf_op jit(solution)/shard_map/reshape | solution.py:156
  265.4 14.5 %reshape.287 = bf16[32,3,60,160]{3,0,2,1:T(8,128)(2,1)} reshape(bf16[32,3,2,30,8,20]{5,4,0,3,2,1:T(8,128)(2,1)} %copy.50) | data formatting | bytes 3686400 | tf_op jit(solution)/shard_map/reshape | solution.py:156
  (62 shorter events, 7.5 us)
Async XLA Ops:
  2.1 6.5 %collective-permute-start = (bf16[32,1,160]{2,0,1:T(8,128)(2,1)S(1)}, bf16[32,1,160]{2,0,1:T(8,128)(2,1)S(1)}, u32[]{:S(2)}, u32[]{:S(2)}) collective-permute-start(bf16[32,1,160]{2,0,1:T(8,128)(2,1)S(1)} %get-tuple-element.15), channel_id=1, source_target_pairs={{1,0},{2,1},{3,2},{0,3},{5,4},{6,5},{7,6},{4,7},{9,8},{10,9},{11,1... | collective-permute-start | bytes 30728 | tf_op jit(solution)/shard_map/ppermute | solution.py:22
  7.2 5.5 %collective-permute-start.1 = (bf16[32,1,160]{2,0,1:T(8,128)(2,1)S(1)}, bf16[32,1,160]{2,0,1:T(8,128)(2,1)S(1)}, u32[]{:S(2)}, u32[]{:S(2)}) collective-permute-start(bf16[32,1,160]{2,0,1:T(8,128)(2,1)S(1)} %get-tuple-element.16), channel_id=1, source_target_pairs={{0,1},{1,2},{2,3},{3,0},{4,5},{5,6},{6,7},{7,4},{8,9},{9,10},{10,1... | collective-permute-start | bytes 30728 | tf_op jit(solution)/shard_map/ppermute | solution.py:20
  14.8 4.0 %copy-start.1 = (bf16[32,60,160]{2,0,1:T(8,128)(2,1)}, bf16[32,60,160]{2,0,1:T(8,128)(2,1)S(1)}, u32[]{:S(2)}) copy-start(bf16[32,60,160]{2,0,1:T(8,128)(2,1)S(1)} %fusion.11) | copy-start | bytes 1843204
  14.8 10.6 %collective-permute-start.2 = (bf16[32,1,160]{2,0,1:T(8,128)(2,1)S(1)}, bf16[32,1,160]{2,0,1:T(8,128)(2,1)S(1)}, u32[]{:S(2)}, u32[]{:S(2)}) collective-permute-start(bf16[32,1,160]{2,0,1:T(8,128)(2,1)S(1)} %get-tuple-element.13), channel_id=1, source_target_pairs={{0,1},{1,2},{2,3},{3,0},{4,5},{5,6},{6,7},{7,4},{8,9},{9,10},{10,1... | collective-permute-start | bytes 30728 | tf_op jit(solution)/shard_map/ppermute | solution.py:20
  14.9 10.5 %collective-permute-start.3 = (bf16[32,1,160]{2,0,1:T(8,128)(2,1)S(1)}, bf16[32,1,160]{2,0,1:T(8,128)(2,1)S(1)}, u32[]{:S(2)}, u32[]{:S(2)}) collective-permute-start(bf16[32,1,160]{2,0,1:T(8,128)(2,1)S(1)} %get-tuple-element.14), channel_id=1, source_target_pairs={{1,0},{2,1},{3,2},{0,3},{5,4},{6,5},{7,6},{4,7},{9,8},{10,9},{11,1... | collective-permute-start | bytes 30728 | tf_op jit(solution)/shard_map/ppermute | solution.py:22
  26.9 1.8 copy-start.2
  99.7 4.0 %copy-start.3 = (s32[1,2,512]{2,1,0:T(2,128)S(1)}, s32[1,2,512]{2,1,0:T(2,128)}, u32[]{:S(2)}) copy-start(s32[1,2,512]{2,1,0:T(2,128)} %param.8) | copy-start | bytes 12292
  99.7 29.1 %all-to-all-start = ((bf16[8,2,32,1800]{3,2,1,0:T(8,128)(2,1)}), bf16[8,2,32,1800]{3,2,1,0:T(8,128)(2,1)S(1)}, u32[]{:S(2)}, u32[]{:S(2)}) async-start(bf16[8,2,32,1800]{3,2,1,0:T(8,128)(2,1)} %copy.34), calls=%async_computation | async-start | bytes 3932160 | tf_op jit(solution)/shard_map/all_to_all | solution.py:101
  128.8 2.0 copy-start
  133.6 6.2 %copy-start.4 = (f32[1,2,512]{2,1,0:T(2,128)S(1)}, f32[1,2,512]{2,1,0:T(2,128)}, u32[]{:S(2)}) copy-start(f32[1,2,512]{2,1,0:T(2,128)} %param.10) | copy-start | bytes 12292
  133.6 6.2 %copy-start.6 = (s32[1,2]{1,0:T(1,128)S(1)}, s32[1,2]{1,0:T(1,128)}, u32[]{:S(2)}) copy-start(s32[1,2]{1,0:T(1,128)} %param.11) | copy-start | bytes 28
  139.5 1.2 copy-start.5
  140.1 12.4 %collective-permute-start.5 = (bf16[1,2,256,512]{3,2,1,0:T(8,128)(2,1)S(1)}, bf16[1,2,256,512]{3,2,1,0:T(8,128)(2,1)S(1)}, u32[]{:S(2)}, u32[]{:S(2)}) collective-permute-start(bf16[1,2,256,512]{3,2,1,0:T(8,128)(2,1)S(1)} %multiply_convert_fusion), channel_id=1, source_target_pairs={{4,0},{8,4},{12,8},{16,12},{20,16},{24,20},{28,24},{0,28},{5,1},{9... | collective-permute-start | bytes 1572872 | tf_op jit(solution)/shard_map/ppermute | solution.py:22
  140.1 13.4 %collective-permute-start.4 = (bf16[1,2,256,512]{3,2,1,0:T(8,128)(2,1)S(1)}, bf16[1,2,256,512]{3,2,1,0:T(8,128)(2,1)S(1)}, u32[]{:S(2)}, u32[]{:S(2)}) collective-permute-start(bf16[1,2,256,512]{3,2,1,0:T(8,128)(2,1)S(1)} %multiply_convert_fusion), channel_id=1, source_target_pairs={{0,4},{4,8},{8,12},{12,16},{16,20},{20,24},{24,28},{28,0},{1,5},{5... | collective-permute-start | bytes 1572872 | tf_op jit(solution)/shard_map/ppermute | solution.py:20
  140.8 17.0 %collective-permute-start.9 = (bf16[1,2,512]{2,1,0:T(2,128)(2,1)S(1)}, bf16[1,2,512]{2,1,0:T(2,128)(2,1)S(1)}, u32[]{:S(2)}, u32[]{:S(2)}) collective-permute-start(bf16[1,2,512]{2,1,0:T(2,128)(2,1)S(1)} %fusion.45), channel_id=1, source_target_pairs={{4,0},{8,4},{12,8},{16,12},{20,16},{24,20},{28,24},{0,28},{5,1},{9... | collective-permute-start | bytes 6152 | tf_op jit(solution)/shard_map/ppermute | solution.py:22
  143.0 14.7 %collective-permute-start.8 = (bf16[1,2,512]{2,1,0:T(2,128)(2,1)S(1)}, bf16[1,2,512]{2,1,0:T(2,128)(2,1)S(1)}, u32[]{:S(2)}, u32[]{:S(2)}) collective-permute-start(bf16[1,2,512]{2,1,0:T(2,128)(2,1)S(1)} %fusion.45), channel_id=1, source_target_pairs={{0,4},{4,8},{8,12},{12,16},{16,20},{20,24},{24,28},{28,0},{1,5},{5... | collective-permute-start | bytes 6152 | tf_op jit(solution)/shard_map/ppermute | solution.py:20
  153.9 37.5 %collective-permute-start.6 = (bf16[3,1,256,512]{3,2,1,0:T(8,128)(2,1)S(1)}, bf16[3,1,256,512]{3,2,1,0:T(8,128)(2,1)S(1)}, u32[]{:S(2)}, u32[]{:S(2)}) collective-permute-start(bf16[3,1,256,512]{3,2,1,0:T(8,128)(2,1)S(1)} %get-tuple-element.11), channel_id=1, source_target_pairs={{0,1},{1,2},{2,3},{3,0},{4,5},{5,6},{6,7},{7,4},{8,9},{9,10},{10,1... | collective-permute-start | bytes 2359304 | tf_op jit(solution)/shard_map/ppermute | solution.py:20
  153.9 37.4 %collective-permute-start.7 = (bf16[3,1,256,512]{3,2,1,0:T(8,128)(2,1)S(1)}, bf16[3,1,256,512]{3,2,1,0:T(8,128)(2,1)S(1)}, u32[]{:S(2)}, u32[]{:S(2)}) collective-permute-start(bf16[3,1,256,512]{3,2,1,0:T(8,128)(2,1)S(1)} %get-tuple-element.12), channel_id=1, source_target_pairs={{1,0},{2,1},{3,2},{0,3},{5,4},{6,5},{7,6},{4,7},{9,8},{10,9},{11,1... | collective-permute-start | bytes 2359304 | tf_op jit(solution)/shard_map/ppermute | solution.py:22
  157.8 33.5 %collective-permute-start.10 = (bf16[3,1,512]{2,1,0:T(2,128)(2,1)S(1)}, bf16[3,1,512]{2,1,0:T(2,128)(2,1)S(1)}, u32[]{:S(2)}, u32[]{:S(2)}) collective-permute-start(bf16[3,1,512]{2,1,0:T(2,128)(2,1)S(1)} %get-tuple-element.17), channel_id=1, source_target_pairs={{0,1},{1,2},{2,3},{3,0},{4,5},{5,6},{6,7},{7,4},{8,9},{9,10},{10,1... | collective-permute-start | bytes 9224 | tf_op jit(solution)/shard_map/ppermute | solution.py:20
  157.9 33.4 %collective-permute-start.11 = (bf16[3,1,512]{2,1,0:T(2,128)(2,1)S(1)}, bf16[3,1,512]{2,1,0:T(2,128)(2,1)S(1)}, u32[]{:S(2)}, u32[]{:S(2)}) collective-permute-start(bf16[3,1,512]{2,1,0:T(2,128)(2,1)S(1)} %get-tuple-element.18), channel_id=1, source_target_pairs={{1,0},{2,1},{3,2},{0,3},{5,4},{6,5},{7,6},{4,7},{9,8},{10,9},{11,1... | collective-permute-start | bytes 9224 | tf_op jit(solution)/shard_map/ppermute | solution.py:22
where the time goes:
time: 282 us; the launch traced here: 280 us
  local copies, waits for them, and re-layouts  115 us (41%)
  waiting for transfers between devices  68.4 us (24%)
  other arithmetic  28.9 us (10%)
  blocking collectives  28.6 us (10%)
  starting transfers between devices  23.5 us (8%)
  matrix products  15.1 us (5%)
    ppermute x6, waiting for transfers between devices, padded_2(): lax.ppermute(tail, axis, [(i, (i + 1) % count) for i in range(count)])  34.8 us
    reshape x2, local copies, waits for them, and re-layouts, on_device(): jnp.transpose(returned, (2, 3, 1, 4, 0, 5))  31.3 us
    all_to_all x1, blocking collectives, on_device(): lax.all_to_all(analysed[None], 'mem', split_axis=2, concat_axis=0, tiled=...  28.6 us
    all_to_all x1, waiting for transfers between devices, on_device(): lax.all_to_all(reordered, 'mem', split_axis=0, concat_axis=2, tiled=True)[0]  25 us
    transpose x1, local copies, waits for them, and re-layouts, on_device(): jnp.transpose(reordered, (4, 2, 0, 1, 3, 5))  24.9 us
    ppermute x6, starting transfers between devices, padded_2(): lax.ppermute(head, axis, [((i + 1) % count, i) for i in range(count)])  18.8 us
    transpose x1, other arithmetic, on_device(): jnp.transpose(reordered, (4, 2, 0, 1, 3, 5))  17 us
    another operation x3, local copies, waits for them, and re-layouts, on_device(): jnp.stack([surface_elevation_cast, revised_zonal_velocity.astype(jnp.bflo...  15.8 us
  transfers between devices with their start and end apart: 13, of which 6 were waited for; matrix products, arithmetic and copies ran while one was open for 3% of the time, Pallas kernels for 0%

commit v1 on v0

--- a/solution.py
+++ b/solution.py
@@ -98,7 +98,10 @@
     reordered = jnp.transpose(reordered, (4, 2, 0, 1, 3, 5)).reshape(
         strips, tile_count, block_members, tile_cells
     )
-    tile_block = lax.all_to_all(reordered, "mem", split_axis=0, concat_axis=2, tiled=True)[0]
+    tile_block = jnp.concatenate(
+        lax.all_to_all(jnp.stack(jnp.split(reordered, lax.axis_size("mem"), axis=0)), "mem", 0, 0),
+        axis=2,
+    )[0]
     cells_here = observed_cell[0]
     values = jnp.take_along_axis(tile_block, cells_here[:, None, :], axis=2)
     observed_mean = jnp.sum(values, axis=1, dtype=jnp.float32) / members

time: 282 us -> 308 us (1.092)
  local copies, waits for them, and re-layouts: 115 us -> 137 us
    split x0 -> x9, local copies, waits for them, and re-layouts: none -> 32.7 us  [on_device(): jnp.split(reordered, lax.axis_size('mem'), axis=0)]
    transpose x1 -> x0, local copies, waits for them, and re-layouts: 24.9 us -> none  [on_device(): jnp.transpose(reordered, (4, 2, 0, 1, 3, 5))]
    another operation x0 -> x10, local copies, waits for them, and re-layouts: none -> 20.7 us  [the longest x9 17.8 us: on_device(): jnp.stack(jnp.split(reordered, lax.axis_size('mem'), axis=0))]
    reshape x1, local copies, waits for them, and re-layouts: 9.05 us -> 2.97 us  [on_device(): jnp.concatenate(lax.all_to_all(jnp.stack(jnp.split(reordered, lax.axis_si...]
    unnamed x15 -> x32, local copies, waits for them, and re-layouts: 2.09 us -> 6.64 us
where the time goes in v1:
time: 308 us; the launch traced here: 303 us
  local copies, waits for them, and re-layouts  137 us (44%)
  waiting for transfers between devices  68.3 us (22%)
  blocking collectives  28.6 us (9%)
  other arithmetic  28.2 us (9%)
  starting transfers between devices  24.7 us (8%)
  matrix products  15.2 us (5%)
    ppermute x6, waiting for transfers between devices, padded_2(): lax.ppermute(tail, axis, [(i, (i + 1) % count) for i in range(count)])  34.6 us
    split x9, local copies, waits for them, and re-layouts, on_device(): jnp.split(reordered, lax.axis_size('mem'), axis=0)  32.7 us
    reshape x2, local copies, waits for them, and re-layouts, on_device(): jnp.transpose(returned, (2, 3, 1, 4, 0, 5))  31.3 us
    all_to_all x1, blocking collectives, on_device(): lax.all_to_all(analysed[None], 'mem', split_axis=2, concat_axis=0, tiled=...  28.6 us
    all_to_all x1, waiting for transfers between devices, on_device(): lax.all_to_all(jnp.stack(jnp.split(reordered, lax.axis_size('mem'), axis=...  25.1 us
    ppermute x6, starting transfers between devices, padded_2(): lax.ppermute(head, axis, [((i + 1) % count, i) for i in range(count)])  19.6 us
    another operation x9, local copies, waits for them, and re-layouts, on_device(): jnp.stack(jnp.split(reordered, lax.axis_size('mem'), axis=0))  17.8 us
    transpose x1, other arithmetic, on_device(): jnp.transpose(reordered, (4, 2, 0, 1, 3, 5))  16.2 us
  transfers between devices with their start and end apart: 13, of which 6 were waited for; matrix products, arithmetic and copies ran while one was open for 3% of the time, Pallas kernels for 0%

profile of v1, /device:TPU:0, one launch (start us, length us, event | category | flops | bytes accessed | tf_op | source)
XLA Modules:
  0.0 303.4 jit_solution(4088305750039314317)
XLA Ops:
  0.0 2.0 fusion.1
  2.1 5.1 %collective-permute-start = (bf16[32,1,160]{2,0,1:T(8,128)(2,1)S(1)}, bf16[32,1,160]{2,0,1:T(8,128)(2,1)S(1)}, u32[]{:S(2)}, u32[]{:S(2)}) collective-permute-start(bf16[32,1,160]{2,0,1:T(8,128)(2,1)S(1)} %get-tuple-element.23), channel_id=1, source_target_pairs={{1,0},{2,1},{3,2},{0,3},{5,4},{6,5},{7,6},{4,7},{9,8},{10,9},{11,1... | collective-permute-start | bytes 30728 | tf_op jit(solution)/shard_map/ppermute | solution.py:22
  8.6 4.1 %collective-permute-done.1 = bf16[32,1,160]{2,0,1:T(8,128)(2,1)S(1)} collective-permute-done((bf16[32,1,160]{2,0,1:T(8,128)(2,1)S(1)}, bf16[32,1,160]{2,0,1:T(8,128)(2,1)S(1)}, u32[]{:S(2)}, u32[]{:S(2)}) %collective-permute-start.1) | collective-permute-done | bytes 10272 | tf_op jit(solution)/shard_map/ppermute | solution.py:20
  12.7 2.1 fusion.11
  14.9 4.3 %collective-permute-start.3 = (bf16[32,1,160]{2,0,1:T(8,128)(2,1)S(1)}, bf16[32,1,160]{2,0,1:T(8,128)(2,1)S(1)}, u32[]{:S(2)}, u32[]{:S(2)}) collective-permute-start(bf16[32,1,160]{2,0,1:T(8,128)(2,1)S(1)} %get-tuple-element.22), channel_id=1, source_target_pairs={{1,0},{2,1},{3,2},{0,3},{5,4},{6,5},{7,6},{4,7},{9,8},{10,9},{11,1... | collective-permute-start | bytes 30728 | tf_op jit(solution)/shard_map/ppermute | solution.py:22
  19.3 2.1 copy.53
  21.4 4.6 %stack.39 = bf16[32,1,2,30,8,20]{3,2,5,4,0,1:T(2,128)(2,1)S(1)} reshape(bf16[32,60,160]{1,2,0:T(8,128)(2,1)} %copy.53) | data formatting | bytes 1228800 | tf_op jit(solution)/shard_map/stack | solution.py:87
  27.6 1.6 copy-done.1
  29.2 2.6 fusion.3
  31.9 3.0 %copy.54 = bf16[32,60,160]{1,2,0:T(8,128)(2,1)} copy(bf16[32,60,160]{2,0,1:T(8,128)(2,1)} %get-tuple-element.17) | data formatting | bytes 1228800 | tf_op jit(solution)/shard_map/convert_element_type | solution.py:90
  34.9 5.6 %stack.40 = bf16[32,1,2,30,8,20]{3,2,5,4,0,1:T(2,128)(2,1)} reshape(bf16[32,60,160]{1,2,0:T(8,128)(2,1)} %copy.54) | data formatting | bytes 1228800 | tf_op jit(solution)/shard_map/stack | solution.py:87
  40.5 3.0 %copy.55 = bf16[32,60,160]{1,2,0:T(8,128)(2,1)} copy(bf16[32,60,160]{2,0,1:T(8,128)(2,1)} %get-tuple-element.18) | data formatting | bytes 1228800 | tf_op jit(solution)/shard_map/convert_element_type | solution.py:91
  43.6 5.6 %stack.41 = bf16[32,1,2,30,8,20]{3,2,5,4,0,1:T(2,128)(2,1)} reshape(bf16[32,60,160]{1,2,0:T(8,128)(2,1)} %copy.55) | data formatting | bytes 1228800 | tf_op jit(solution)/shard_map/stack | solution.py:87
  49.2 16.2 %maximum_bitcast_fusion = bf16[8,2,32,3,30,20]{4,1,5,0,2,3:T(2,128)(2,1)S(1)} fusion(bf16[32,1,2,30,8,20]{3,2,5,4,0,1:T(2,128)(2,1)} %stack.41, bf16[32,1,2,30,8,20]{3,2,5,4,0,1:T(2,128)(2,1)} %stack.40, bf16[32,1,2,30,8,20]{3,2,5,4,0,1:T(2,128)(2,1)S(1)} %stack.39), kind=kLoop, calls=%fused_computation.1 | loop fusion | flops 1843200 | bytes 3686400 | tf_op jit(solution)/shard_map/transpose | solution.py:98
  65.4 9.2 %fusion.60 = (bf16[1,2,32,3,30,20]{4,1,5,0,2,3:T(2,128)(2,1)}, bf16[1,2,32,3,30,20]{4,1,5,0,2,3:T(2,128)(2,1)}, bf16[1,2,32,3,30,20]{4,1,5,0,2,3:T(2,128)(2,1)},...) fusion(bf16[8,2,32,3,30,20]{4,1,5,0,2,3:T(2,128)(2,1)S(1)} %max, ...), kind=kLoop, calls=%fused_computation.133 | loop fusion | bytes 3686400 | tf_op jit(solution)/shard_map/split | solution.py:102
  74.6 3.4 %copy.63 = bf16[1,2,32,3,30,20]{5,4,3,2,1,0:T(8,128)(2,1)S(1)} copy(bf16[1,2,32,3,30,20]{4,1,5,0,2,3:T(2,128)(2,1)} %get-tuple-element.7) | data formatting | bytes 460800 | tf_op jit(solution)/shard_map/split | solution.py:102
  78.0 2.3 stack.50
  80.3 3.2 %copy.62 = bf16[1,2,32,3,30,20]{5,4,3,2,1,0:T(8,128)(2,1)S(1)} copy(bf16[1,2,32,3,30,20]{4,1,5,0,2,3:T(2,128)(2,1)} %get-tuple-element.8) | data formatting | bytes 460800 | tf_op jit(solution)/shard_map/split | solution.py:102
  83.6 2.3 stack.49
  85.9 3.2 %copy.61 = bf16[1,2,32,3,30,20]{5,4,3,2,1,0:T(8,128)(2,1)S(1)} copy(bf16[1,2,32,3,30,20]{4,1,5,0,2,3:T(2,128)(2,1)} %get-tuple-element.9) | data formatting | bytes 460800 | tf_op jit(solution)/shard_map/split | solution.py:102
  89.1 2.3 stack.48
  91.5 3.2 %copy.60 = bf16[1,2,32,3,30,20]{5,4,3,2,1,0:T(8,128)(2,1)S(1)} copy(bf16[1,2,32,3,30,20]{4,1,5,0,2,3:T(2,128)(2,1)} %get-tuple-element.10) | data formatting | bytes 460800 | tf_op jit(solution)/shard_map/split | solution.py:102
  94.7 2.3 stack.47
  97.0 3.2 %copy.59 = bf16[1,2,32,3,30,20]{5,4,3,2,1,0:T(8,128)(2,1)S(1)} copy(bf16[1,2,32,3,30,20]{4,1,5,0,2,3:T(2,128)(2,1)} %get-tuple-element.11) | data formatting | bytes 460800 | tf_op jit(solution)/shard_map/split | solution.py:102
  100.3 2.3 stack.46
  102.6 3.2 %copy.58 = bf16[1,2,32,3,30,20]{5,4,3,2,1,0:T(8,128)(2,1)S(1)} copy(bf16[1,2,32,3,30,20]{4,1,5,0,2,3:T(2,128)(2,1)} %get-tuple-element.12) | data formatting | bytes 460800 | tf_op jit(solution)/shard_map/split | solution.py:102
  105.8 2.3 stack.45
  108.2 2.1 copy.57
  110.2 1.6 stack.44
  111.8 1.8 copy.56
  113.7 1.6 stack.43
  121.0 4.5 %all-to-all-start = ((bf16[8,1,2,32,1800]{4,3,2,1,0:T(8,128)(2,1)}), bf16[8,1,2,32,1800]{4,3,2,1,0:T(8,128)(2,1)}, u32[]{:S(2)}, u32[]{:S(2)}) async-start(bf16[8,1,2,32,1800]{4,3,2,1,0:T(8,128)(2,1)} %constant_dynamic-update-slice_fusion), calls=%async_computation | async-start | bytes 3932160 | tf_op jit(solution)/shard_map/all_to_all | solution.py:102
  125.7 25.1 %all-to-all-done = bf16[8,1,2,32,1800]{4,3,2,1,0:T(8,128)(2,1)} async-done(((bf16[8,1,2,32,1800]{4,3,2,1,0:T(8,128)(2,1)}), bf16[8,1,2,32,1800]{4,3,2,1,0:T(8,128)(2,1)}, u32[]{:S(2)}, u32[]{:S(2)}) %all-to-all-start) | async-done | bytes 1843232 | tf_op jit(solution)/shard_map/all_to_all | solution.py:102
  150.8 3.0 copy.64
  153.7 2.8 copy.65
  156.6 5.8 %gather_fusion = bf16[1024,256]{1,0:T(8,128)(2,1)S(1)} fusion(bf16[2,256,1800]{1,2,0:T(8,128)(2,1)S(1)} %copy.65, s32[1024]{0:T(1024)S(1)} %bitcast.110), kind=kCustom, calls=%fused_computation | custom fusion | bytes 1056768 | tf_op jit(solution)/shard_map/jit(take_along_axis)/gather | solution.py:106
  163.7 2.3 collective-permute-start.9
  166.0 1.9 convert_reduce_fusion
  167.9 7.6 %collective-permute-done.5 = bf16[1,2,256,512]{3,2,1,0:T(8,128)(2,1)S(1)} collective-permute-done((bf16[1,2,256,512]{3,2,1,0:T(8,128)(2,1)S(1)}, bf16[1,2,256,512]{3,2,1,0:T(8,128)(2,1)S(1)}, u32[]{:S(2)}, u32[]{:S(2)}) %collective-permute-start.5) | collective-permute-done | bytes 524320 | tf_op jit(solution)/shard_map/ppermute | solution.py:22
  176.9 3.8 %collective-permute-start.7 = (bf16[3,1,256,512]{3,2,1,0:T(8,128)(2,1)S(1)}, bf16[3,1,256,512]{3,2,1,0:T(8,128)(2,1)S(1)}, u32[]{:S(2)}, u32[]{:S(2)}) collective-permute-start(bf16[3,1,256,512]{3,2,1,0:T(8,128)(2,1)S(1)} %get-tuple-element.20), channel_id=1, source_target_pairs={{1,0},{2,1},{3,2},{0,3},{5,4},{6,5},{7,6},{4,7},{9,8},{10,9},{11,1... | collective-permute-start | bytes 2359304 | tf_op jit(solution)/shard_map/ppermute | solution.py:22
  180.8 4.0 %collective-permute-start.11 = (bf16[3,1,512]{2,1,0:T(2,128)(2,1)S(1)}, bf16[3,1,512]{2,1,0:T(2,128)(2,1)S(1)}, u32[]{:S(2)}, u32[]{:S(2)}) collective-permute-start(bf16[3,1,512]{2,1,0:T(2,128)(2,1)S(1)} %get-tuple-element.26), channel_id=1, source_target_pairs={{1,0},{2,1},{3,2},{0,3},{5,4},{6,5},{7,6},{4,7},{9,8},{10,9},{11,1... | collective-permute-start | bytes 9224 | tf_op jit(solution)/shard_map/ppermute | solution.py:22
  184.8 29.4 %collective-permute-done.10 = bf16[3,1,512]{2,1,0:T(2,128)(2,1)S(1)} collective-permute-done((bf16[3,1,512]{2,1,0:T(2,128)(2,1)S(1)}, bf16[3,1,512]{2,1,0:T(2,128)(2,1)S(1)}, u32[]{:S(2)}, u32[]{:S(2)}) %collective-permute-start.10) | collective-permute-done | bytes 3104 | tf_op jit(solution)/shard_map/ppermute | solution.py:20
  228.1 2.2 fusion
  230.2 5.1 %copy.68 = bf16[1,2,256,1800]{3,1,0,2:T(2,128)(2,1)S(1)} copy(bf16[1,2,256,1800]{2,3,1,0:T(8,128)(2,1)} %fusion) | data formatting | bytes 3686400 | tf_op jit(solution)/shard_map/broadcast_in_dim | solution.py:157
  235.3 28.6 %all_to_all.20 = bf16[1,2,256,1800]{3,1,0,2:T(2,128)(2,1)S(1)} all-to-all(bf16[1,2,256,1800]{3,1,0,2:T(2,128)(2,1)S(1)} %copy.68), channel_id=1, replica_groups=mesh['mem'=8,'band'=4] {'mem'}, dimensions={2} | all-to-all | bytes 3686400 | tf_op jit(solution)/shard_map/all_to_all | solution.py:157
  264.1 7.5 %copy.70 = bf16[8,1,2,32,1800]{3,0,4,2,1:T(8,128)(2,1)} copy(bf16[8,1,2,32,1800]{4,3,0,2,1:T(8,128)(2,1)S(1)} %bitcast.112) | data formatting | bytes 3686400 | tf_op jit(solution)/shard_map/all_to_all | solution.py:157
  271.6 16.8 %copy.79 = bf16[32,3,2,30,8,20]{5,4,0,3,2,1:T(8,128)(2,1)} copy(bf16[32,3,2,30,8,20]{0,4,5,3,1,2:T(8,128)(2,1)} %bitcast.111) | data formatting | bytes 3686400 | tf_op jit(solution)/shard_map/reshape | solution.py:159
  288.4 14.5 %reshape.303 = bf16[32,3,60,160]{3,0,2,1:T(8,128)(2,1)} reshape(bf16[32,3,2,30,8,20]{5,4,0,3,2,1:T(8,128)(2,1)} %copy.79) | data formatting | bytes 3686400 | tf_op jit(solution)/shard_map/reshape | solution.py:159
  (95 shorter events, 25.7 us)
Async XLA Ops:
  2.1 6.5 %collective-permute-start = (bf16[32,1,160]{2,0,1:T(8,128)(2,1)S(1)}, bf16[32,1,160]{2,0,1:T(8,128)(2,1)S(1)}, u32[]{:S(2)}, u32[]{:S(2)}) collective-permute-start(bf16[32,1,160]{2,0,1:T(8,128)(2,1)S(1)} %get-tuple-element.23), channel_id=1, source_target_pairs={{1,0},{2,1},{3,2},{0,3},{5,4},{6,5},{7,6},{4,7},{9,8},{10,9},{11,1... | collective-permute-start | bytes 30728 | tf_op jit(solution)/shard_map/ppermute | solution.py:22
  7.2 5.5 %collective-permute-start.1 = (bf16[32,1,160]{2,0,1:T(8,128)(2,1)S(1)}, bf16[32,1,160]{2,0,1:T(8,128)(2,1)S(1)}, u32[]{:S(2)}, u32[]{:S(2)}) collective-permute-start(bf16[32,1,160]{2,0,1:T(8,128)(2,1)S(1)} %get-tuple-element.24), channel_id=1, source_target_pairs={{0,1},{1,2},{2,3},{3,0},{4,5},{5,6},{6,7},{7,4},{8,9},{9,10},{10,1... | collective-permute-start | bytes 30728 | tf_op jit(solution)/shard_map/ppermute | solution.py:20
  14.8 4.5 %copy-start = (bf16[32,60,160]{2,0,1:T(8,128)(2,1)}, bf16[32,60,160]{2,0,1:T(8,128)(2,1)S(1)}, u32[]{:S(2)}) copy-start(bf16[32,60,160]{2,0,1:T(8,128)(2,1)S(1)} %fusion.11) | copy-start | bytes 1843204
  14.8 11.1 %collective-permute-start.2 = (bf16[32,1,160]{2,0,1:T(8,128)(2,1)S(1)}, bf16[32,1,160]{2,0,1:T(8,128)(2,1)S(1)}, u32[]{:S(2)}, u32[]{:S(2)}) collective-permute-start(bf16[32,1,160]{2,0,1:T(8,128)(2,1)S(1)} %get-tuple-element.21), channel_id=1, source_target_pairs={{0,1},{1,2},{2,3},{3,0},{4,5},{5,6},{6,7},{7,4},{8,9},{9,10},{10,1... | collective-permute-start | bytes 30728 | tf_op jit(solution)/shard_map/ppermute | solution.py:20
  14.9 11.0 %collective-permute-start.3 = (bf16[32,1,160]{2,0,1:T(8,128)(2,1)S(1)}, bf16[32,1,160]{2,0,1:T(8,128)(2,1)S(1)}, u32[]{:S(2)}, u32[]{:S(2)}) collective-permute-start(bf16[32,1,160]{2,0,1:T(8,128)(2,1)S(1)} %get-tuple-element.22), channel_id=1, source_target_pairs={{1,0},{2,1},{3,2},{0,3},{5,4},{6,5},{7,6},{4,7},{9,8},{10,9},{11,1... | collective-permute-start | bytes 30728 | tf_op jit(solution)/shard_map/ppermute | solution.py:22
  27.4 1.8 copy-start.1
  113.7 3.1 %copy-start.7 = (bf16[1,1,2,32,1800]{4,3,2,1,0:T(8,128)(2,1)S(1)}, bf16[1,1,2,32,1800]{4,3,2,1,0:T(8,128)(2,1)}, u32[]{:S(2)}) copy-start(bf16[1,1,2,32,1800]{4,3,2,1,0:T(8,128)(2,1)} %stack.45) | copy-start | bytes 691204
  113.7 3.8 %copy-start.6 = (bf16[1,1,2,32,1800]{4,3,2,1,0:T(8,128)(2,1)S(1)}, bf16[1,1,2,32,1800]{4,3,2,1,0:T(8,128)(2,1)}, u32[]{:S(2)}) copy-start(bf16[1,1,2,32,1800]{4,3,2,1,0:T(8,128)(2,1)} %stack.46) | copy-start | bytes 691204
  113.7 4.5 %copy-start.5 = (bf16[1,1,2,32,1800]{4,3,2,1,0:T(8,128)(2,1)S(1)}, bf16[1,1,2,32,1800]{4,3,2,1,0:T(8,128)(2,1)}, u32[]{:S(2)}) copy-start(bf16[1,1,2,32,1800]{4,3,2,1,0:T(8,128)(2,1)} %stack.47) | copy-start | bytes 691204
  113.7 5.2 %copy-start.4 = (bf16[1,1,2,32,1800]{4,3,2,1,0:T(8,128)(2,1)S(1)}, bf16[1,1,2,32,1800]{4,3,2,1,0:T(8,128)(2,1)}, u32[]{:S(2)}) copy-start(bf16[1,1,2,32,1800]{4,3,2,1,0:T(8,128)(2,1)} %stack.48) | copy-start | bytes 691204
  113.7 5.9 %copy-start.3 = (bf16[1,1,2,32,1800]{4,3,2,1,0:T(8,128)(2,1)S(1)}, bf16[1,1,2,32,1800]{4,3,2,1,0:T(8,128)(2,1)}, u32[]{:S(2)}) copy-start(bf16[1,1,2,32,1800]{4,3,2,1,0:T(8,128)(2,1)} %stack.49) | copy-start | bytes 691204
  115.3 5.0 %copy-start.2 = (bf16[1,1,2,32,1800]{4,3,2,1,0:T(8,128)(2,1)S(1)}, bf16[1,1,2,32,1800]{4,3,2,1,0:T(8,128)(2,1)}, u32[]{:S(2)}) copy-start(bf16[1,1,2,32,1800]{4,3,2,1,0:T(8,128)(2,1)} %stack.50) | copy-start | bytes 691204
  121.0 4.5 %copy-start.8 = (s32[1,2,512]{2,1,0:T(2,128)S(1)}, s32[1,2,512]{2,1,0:T(2,128)}, u32[]{:S(2)}) copy-start(s32[1,2,512]{2,1,0:T(2,128)} %param.8) | copy-start | bytes 12292
  121.0 29.7 %all-to-all-start = ((bf16[8,1,2,32,1800]{4,3,2,1,0:T(8,128)(2,1)}), bf16[8,1,2,32,1800]{4,3,2,1,0:T(8,128)(2,1)}, u32[]{:S(2)}, u32[]{:S(2)}) async-start(bf16[8,1,2,32,1800]{4,3,2,1,0:T(8,128)(2,1)} %constant_dynamic-update-slice_fusion), calls=%async_computation | async-start | bytes 3932160 | tf_op jit(solution)/shard_map/all_to_all | solution.py:102
  156.6 6.2 %copy-start.9 = (f32[1,2,512]{2,1,0:T(2,128)S(1)}, f32[1,2,512]{2,1,0:T(2,128)}, u32[]{:S(2)}) copy-start(f32[1,2,512]{2,1,0:T(2,128)} %param.10) | copy-start | bytes 12292
  156.6 6.2 %copy-start.11 = (s32[1,2]{1,0:T(1,128)S(1)}, s32[1,2]{1,0:T(1,128)}, u32[]{:S(2)}) copy-start(s32[1,2]{1,0:T(1,128)} %param.11) | copy-start | bytes 28
  162.4 1.2 copy-start.10
  163.1 12.4 %collective-permute-start.5 = (bf16[1,2,256,512]{3,2,1,0:T(8,128)(2,1)S(1)}, bf16[1,2,256,512]{3,2,1,0:T(8,128)(2,1)S(1)}, u32[]{:S(2)}, u32[]{:S(2)}) collective-permute-start(bf16[1,2,256,512]{3,2,1,0:T(8,128)(2,1)S(1)} %multiply_convert_fusion), channel_id=1, source_target_pairs={{4,0},{8,4},{12,8},{16,12},{20,16},{24,20},{28,24},{0,28},{5,1},{9... | collective-permute-start | bytes 1572872 | tf_op jit(solution)/shard_map/ppermute | solution.py:22
  163.1 13.4 %collective-permute-start.4 = (bf16[1,2,256,512]{3,2,1,0:T(8,128)(2,1)S(1)}, bf16[1,2,256,512]{3,2,1,0:T(8,128)(2,1)S(1)}, u32[]{:S(2)}, u32[]{:S(2)}) collective-permute-start(bf16[1,2,256,512]{3,2,1,0:T(8,128)(2,1)S(1)} %multiply_convert_fusion), channel_id=1, source_target_pairs={{0,4},{4,8},{8,12},{12,16},{16,20},{20,24},{24,28},{28,0},{1,5},{5... | collective-permute-start | bytes 1572872 | tf_op jit(solution)/shard_map/ppermute | solution.py:20
  163.7 16.9 %collective-permute-start.9 = (bf16[1,2,512]{2,1,0:T(2,128)(2,1)S(1)}, bf16[1,2,512]{2,1,0:T(2,128)(2,1)S(1)}, u32[]{:S(2)}, u32[]{:S(2)}) collective-permute-start(bf16[1,2,512]{2,1,0:T(2,128)(2,1)S(1)} %fusion.45), channel_id=1, source_target_pairs={{4,0},{8,4},{12,8},{16,12},{20,16},{24,20},{28,24},{0,28},{5,1},{9... | collective-permute-start | bytes 6152 | tf_op jit(solution)/shard_map/ppermute | solution.py:22
  166.0 14.7 %collective-permute-start.8 = (bf16[1,2,512]{2,1,0:T(2,128)(2,1)S(1)}, bf16[1,2,512]{2,1,0:T(2,128)(2,1)S(1)}, u32[]{:S(2)}, u32[]{:S(2)}) collective-permute-start(bf16[1,2,512]{2,1,0:T(2,128)(2,1)S(1)} %fusion.45), channel_id=1, source_target_pairs={{0,4},{4,8},{8,12},{12,16},{16,20},{20,24},{24,28},{28,0},{1,5},{5... | collective-permute-start | bytes 6152 | tf_op jit(solution)/shard_map/ppermute | solution.py:20
  176.8 37.5 %collective-permute-start.6 = (bf16[3,1,256,512]{3,2,1,0:T(8,128)(2,1)S(1)}, bf16[3,1,256,512]{3,2,1,0:T(8,128)(2,1)S(1)}, u32[]{:S(2)}, u32[]{:S(2)}) collective-permute-start(bf16[3,1,256,512]{3,2,1,0:T(8,128)(2,1)S(1)} %get-tuple-element.19), channel_id=1, source_target_pairs={{0,1},{1,2},{2,3},{3,0},{4,5},{5,6},{6,7},{7,4},{8,9},{9,10},{10,1... | collective-permute-start | bytes 2359304 | tf_op jit(solution)/shard_map/ppermute | solution.py:20
  176.9 37.4 %collective-permute-start.7 = (bf16[3,1,256,512]{3,2,1,0:T(8,128)(2,1)S(1)}, bf16[3,1,256,512]{3,2,1,0:T(8,128)(2,1)S(1)}, u32[]{:S(2)}, u32[]{:S(2)}) collective-permute-start(bf16[3,1,256,512]{3,2,1,0:T(8,128)(2,1)S(1)} %get-tuple-element.20), channel_id=1, source_target_pairs={{1,0},{2,1},{3,2},{0,3},{5,4},{6,5},{7,6},{4,7},{9,8},{10,9},{11,1... | collective-permute-start | bytes 2359304 | tf_op jit(solution)/shard_map/ppermute | solution.py:22
  180.7 33.5 %collective-permute-start.10 = (bf16[3,1,512]{2,1,0:T(2,128)(2,1)S(1)}, bf16[3,1,512]{2,1,0:T(2,128)(2,1)S(1)}, u32[]{:S(2)}, u32[]{:S(2)}) collective-permute-start(bf16[3,1,512]{2,1,0:T(2,128)(2,1)S(1)} %get-tuple-element.25), channel_id=1, source_target_pairs={{0,1},{1,2},{2,3},{3,0},{4,5},{5,6},{6,7},{7,4},{8,9},{9,10},{10,1... | collective-permute-start | bytes 9224 | tf_op jit(solution)/shard_map/ppermute | solution.py:20
  180.8 33.4 %collective-permute-start.11 = (bf16[3,1,512]{2,1,0:T(2,128)(2,1)S(1)}, bf16[3,1,512]{2,1,0:T(2,128)(2,1)S(1)}, u32[]{:S(2)}, u32[]{:S(2)}) collective-permute-start(bf16[3,1,512]{2,1,0:T(2,128)(2,1)S(1)} %get-tuple-element.26), channel_id=1, source_target_pairs={{1,0},{2,1},{3,2},{0,3},{5,4},{6,5},{7,6},{4,7},{9,8},{10,9},{11,1... | collective-permute-start | bytes 9224 | tf_op jit(solution)/shard_map/ppermute | solution.py:22
